TPU v7x, 32 devices: a whole 2x2x4 slice. The times are simulated.
32 devices in a mesh: groups: 2 (over y), chan: 4 (over z), tm: 2 (over x), sub: 2 (over core).
Axes of the slice: x: 2, y: 2, z: 4, core: 2. Of those that a mesh axis runs over, the one named last changes fastest.
Arguments:
- traces: float32 [2048, 8192], P(('groups', 'chan', 'sub'), 'tm'), parts along dimension 0, may hold values from -6 to 6
- filters: float32 [2048, 65], P(('groups', 'chan', 'sub')), parts along dimension 0, may hold values from -0.75 to 0.75
- sources: int32 [256], P('groups'), parts along dimension 0, may hold values from 0 to 1023, as said below
Outputs:
- corr: float32 [128, 129, 2048], P('tm', None, ('groups', 'chan', 'sub')), parts along dimension 2
There are 2 independent parts, one for each index of `groups`. A program takes and returns all parts, laid end to end along the dimension named above; each array names one. Nothing has to cross between parts.
Inputs may be any that keep to these rules, and one draw needn't show every extreme that they name: `sources`: the 128 partner channels are distinct. No block of 128 consecutive channels starting at a multiple of 128 holds more than 16 of them, and some block holds exactly 16.
All inputs are finite; a program needn't handle non-finite values.
Results may differ from a plain program's by a relative error of at most 0.0033.
Values may be sent and summed in bfloat16 or wider, within the bound.
A program may use at most 64 MiB of HBM per device.

v0:
```python
import math
import jax
import jax.numpy as jnp
from jax import lax
from jax.sharding import PartitionSpec as P

LAGS = 129


def padded_2(block, sides, width):
    for axis, dim in sides:
        count = lax.axis_size(axis)
        forward = [(i, i + 1) for i in range(count - 1)]
        backward = [(target, source) for source, target in forward]
        low = lax.ppermute(
            lax.slice_in_dim(block, block.shape[dim] - width, None, axis=dim), axis, forward
        )
        high = lax.ppermute(lax.slice_in_dim(block, 0, width, axis=dim), axis, backward)
        block = jnp.concatenate([low, block, high], axis=dim)
    return block


def whiten(extended, filters, out_len):
    running = jnp.zeros((extended.shape[0], out_len), jnp.float32)
    for k in range(filters.shape[1]):
        running = running + filters[:, k : k + 1] * extended[:, k : k + out_len]
    return running


def correlate(padded_seg, part_rows):
    seg_len = part_rows.shape[1]
    block_len = min(512, seg_len)
    block_count = seg_len // block_len

    def advance(block_index, summed):
        offset = block_index * block_len
        window = lax.dynamic_slice_in_dim(padded_seg, offset, block_len + LAGS - 1, 1)
        rows_here = lax.dynamic_slice_in_dim(part_rows, offset, block_len, 1)
        term = lax.conv_general_dilated(
            window[:, None, :],
            rows_here[:, None, :],
            (1,),
            "VALID",
            dimension_numbers=("NCH", "OIH", "NCH"),
            preferred_element_type=jnp.float32,
        )
        return summed + term

    start_sum = jnp.zeros((padded_seg.shape[0], part_rows.shape[0], LAGS), jnp.float32)
    return lax.fori_loop(0, block_count, advance, start_sum)


def on_device(traces, filters, sources):
    chan_dev, seg_len = traces.shape
    taps = filters.shape[1]
    half_taps = (taps - 1) // 2
    half_lags = (LAGS - 1) // 2
    partner_count = sources.shape[0]
    time_devs = lax.axis_size("tm")
    extended = padded_2(traces, (("tm", 1),), half_taps + half_lags)
    whitened_ext = whiten(extended, filters, seg_len + 2 * half_lags)
    position = (
        lax.axis_index("tm") * seg_len
        - half_lags
        + jnp.arange(seg_len + 2 * half_lags, dtype=jnp.int32)
    )
    inside = (position >= 0) & (position < seg_len * time_devs)
    padded = jnp.where(inside[None, :], whitened_ext, 0.0).astype(jnp.bfloat16)
    whitened = padded[:, half_lags : half_lags + seg_len]
    my_block = lax.axis_index(("chan", "sub"))
    owners = sources // chan_dev
    within = sources % chan_dev
    is_mine = owners == my_block
    chan_ids = jnp.arange(chan_dev, dtype=jnp.int32)
    slot_most = min(chan_dev, partner_count // 8)
    order_ids = jnp.arange(partner_count, dtype=jnp.int32)
    same_owner = owners[:, None] == owners[None, :]
    earlier = order_ids[None, :] < order_ids[:, None]
    rank_in = jnp.sum((same_owner & earlier).astype(jnp.int32), axis=1)
    choose = (
        (rank_in[None, :] == jnp.arange(slot_most, dtype=jnp.int32)[:, None]) & is_mine[None, :]
    ).astype(jnp.bfloat16)
    onehot = (within[:, None] == chan_ids[None, :]).astype(jnp.bfloat16)
    picker = jnp.dot(choose, onehot, preferred_element_type=jnp.float32).astype(jnp.bfloat16)
    slot_rows = jnp.dot(picker, whitened, preferred_element_type=jnp.float32).astype(jnp.bfloat16)
    slot_id = owners * slot_most + rank_in
    segment = lax.all_gather(slot_rows, ("chan", "sub"), axis=0, tiled=True)
    row_count = segment.shape[0]
    select = (slot_id[:, None] == jnp.arange(row_count, dtype=jnp.int32)[None, :]).astype(
        jnp.bfloat16
    )
    partners = jnp.dot(select, segment, preferred_element_type=jnp.float32).astype(jnp.bfloat16)
    norm_scale = 1.0 / math.sqrt(seg_len * time_devs)
    summed = correlate(padded, partners)
    return lax.psum_scatter(
        jnp.transpose(summed[:, :, ::-1], (1, 2, 0)) * norm_scale,
        "tm",
        scatter_dimension=0,
        tiled=True,
    )


def solution(mesh):
    return jax.shard_map(
        on_device,
        mesh=mesh,
        in_specs=(
            P(("groups", "chan", "sub"), "tm"),
            P(("groups", "chan", "sub"), None),
            P("groups"),
        ),
        out_specs=P("tm", None, ("groups", "chan", "sub")),
        check_vma=False,
    )
```

profile of v0, /device:TPU:0, one launch (start us, length us, event | category | flops | bytes accessed | tf_op | source)
XLA Modules:
  0.0 404.3 jit_solution(17135391241325937660)
XLA Ops:
  6.5 1.0 fusion.81
  7.5 1.3 collective-permute-start.1
  8.8 4.9 %collective-permute-start = (f32[128,96]{1,0:T(8,128)S(1)}, f32[128,96]{1,0:T(8,128)S(1)}, u32[]{:S(2)}, u32[]{:S(2)}) collective-permute-start(f32[128,96]{1,0:T(8,128)S(1)} %get-tuple-element.115), channel_id=1, source_target_pairs={{0,2},{1,3},{4,6},{5,7},{8,10},{9,11},{12,14},{13,15},{16,18},{17,... | collective-permute-start | bytes 147464 | tf_op jit(solution)/shard_map/ppermute | solution.py:15
  14.6 1.0 slice_bitcast_fusion.63
  15.6 1.0 slice_bitcast_fusion.64
  16.6 1.0 slice_bitcast_fusion.62
  19.1 2.9 concatenate.3
  22.1 42.9 %fusion.2 = bf16[128,4224]{1,0:T(8,128)(2,1)} fusion(f32[128,4288]{1,0:T(8,128)S(1)} %concatenate.3, f32[128]{0:T(128)S(1)} %get-tuple-element.179, f32[128]{0:T(128)S(1)} %get-tuple-element.180, f32[128]{0:T(128)S(1)} %get-tuple-element.117, f32[128]{0:T(128)S(1)} %get-tuple-element.118, f32[128]{0:T(128)S(1)} %get-tuple-element.119, ...), kind=kLoop, calls=%fused_computation.9 | loop fusion | flops 70828032 | bytes 141693568 | tf_op jit(solution)/shard_map/convert_element_type | solution.py:68
  65.0 2.4 convolution_convert_fusion.1
  67.7 23.6 %all-gather.2.cloned.1.call-done = bf16[128,4096]{1,0:T(8,128)(2,1)} async-done(((bf16[16,4096]{1,0:T(8,128)(2,1)}), bf16[128,4096]{1,0:T(8,128)(2,1)}) %all-gather.2.cloned.1.call-update) | async-done | bytes 1048592 | tf_op jit(solution)/shard_map/all_gather | solution.py:87
  91.3 2.8 convolution_convert_fusion
  94.0 186.1 %while.14 = (s32[]{:T(128)}, f32[128,128,129]{1,0,2:T(8,128)}, bf16[128,4224]{1,0:T(8,128)(2,1)}, bf16[128,4096]{1,0:T(8,128)(2,1)}, s32[]{:T(128)}, /*index=5*/s32[]{:T(128)}, s32[]{:T(128)}, s32[]{:T(128)}, s32[]{:T(128)}) while((s32[]{:T(128)}, f32[128,128,129]{1,0,2:T(8,128)}, bf16[128,4224]{1,0:T(8,128)(2,1)}, ...), condition=%wide.region_2.3_spmd.clone, body=%wide.region_1.2_spmd.clone.sunk | while | flops 2168487936 | bytes 18383036 | solution.py:50
  94.0 0.9 dynamic-slice_bitcast_fusion.5
  95.1 0.9 dynamic-slice_bitcast_fusion.4
  96.3 19.1 %select_add_fusion.2 = f32[128,128,129]{1,0,2:T(8,128)} fusion(f32[128,128,129]{1,0,2:T(8,128)} %get-tuple-element.216, pred[]{:T(512)S(6)} %compare.6, bf16[128,1,640]{0,1,2:T(2,128)(2,1)S(1)} %copy.17, bf16[128,1,512]{0,1,2:T(2,128)(2,1)S(1)} %copy.18), kind=kOutput, calls=%fused_computation.clone.1 | convolution fusion | flops 2168487936 | bytes 17203200 | tf_op jit(solution)/shard_map/while/body/eval_jaxpr/conv_general_dilated | solution.py:39
  116.5 0.9 dynamic-slice_bitcast_fusion.4
  117.6 21.3 %select_add_fusion.2 = f32[128,128,129]{1,0,2:T(8,128)} fusion(f32[128,128,129]{1,0,2:T(8,128)} %get-tuple-element.216, pred[]{:T(512)S(6)} %compare.6, bf16[128,1,640]{0,1,2:T(2,128)(2,1)S(1)} %copy.17, bf16[128,1,512]{0,1,2:T(2,128)(2,1)S(1)} %copy.18), kind=kOutput, calls=%fused_computation.clone.1 | convolution fusion | flops 2168487936 | bytes 17203200 | tf_op jit(solution)/shard_map/while/body/eval_jaxpr/conv_general_dilated | solution.py:39
  140.0 0.9 dynamic-slice_bitcast_fusion.4
  141.2 21.3 %select_add_fusion.2 = f32[128,128,129]{1,0,2:T(8,128)} fusion(f32[128,128,129]{1,0,2:T(8,128)} %get-tuple-element.216, pred[]{:T(512)S(6)} %compare.6, bf16[128,1,640]{0,1,2:T(2,128)(2,1)S(1)} %copy.17, bf16[128,1,512]{0,1,2:T(2,128)(2,1)S(1)} %copy.18), kind=kOutput, calls=%fused_computation.clone.1 | convolution fusion | flops 2168487936 | bytes 17203200 | tf_op jit(solution)/shard_map/while/body/eval_jaxpr/conv_general_dilated | solution.py:39
  163.6 0.9 dynamic-slice_bitcast_fusion.4
  164.7 21.3 %select_add_fusion.2 = f32[128,128,129]{1,0,2:T(8,128)} fusion(f32[128,128,129]{1,0,2:T(8,128)} %get-tuple-element.216, pred[]{:T(512)S(6)} %compare.6, bf16[128,1,640]{0,1,2:T(2,128)(2,1)S(1)} %copy.17, bf16[128,1,512]{0,1,2:T(2,128)(2,1)S(1)} %copy.18), kind=kOutput, calls=%fused_computation.clone.1 | convolution fusion | flops 2168487936 | bytes 17203200 | tf_op jit(solution)/shard_map/while/body/eval_jaxpr/conv_general_dilated | solution.py:39
  187.1 0.9 dynamic-slice_bitcast_fusion.4
  188.3 21.3 %select_add_fusion.2 = f32[128,128,129]{1,0,2:T(8,128)} fusion(f32[128,128,129]{1,0,2:T(8,128)} %get-tuple-element.216, pred[]{:T(512)S(6)} %compare.6, bf16[128,1,640]{0,1,2:T(2,128)(2,1)S(1)} %copy.17, bf16[128,1,512]{0,1,2:T(2,128)(2,1)S(1)} %copy.18), kind=kOutput, calls=%fused_computation.clone.1 | convolution fusion | flops 2168487936 | bytes 17203200 | tf_op jit(solution)/shard_map/while/body/eval_jaxpr/conv_general_dilated | solution.py:39
  210.6 0.9 dynamic-slice_bitcast_fusion.4
  211.8 21.3 %select_add_fusion.2 = f32[128,128,129]{1,0,2:T(8,128)} fusion(f32[128,128,129]{1,0,2:T(8,128)} %get-tuple-element.216, pred[]{:T(512)S(6)} %compare.6, bf16[128,1,640]{0,1,2:T(2,128)(2,1)S(1)} %copy.17, bf16[128,1,512]{0,1,2:T(2,128)(2,1)S(1)} %copy.18), kind=kOutput, calls=%fused_computation.clone.1 | convolution fusion | flops 2168487936 | bytes 17203200 | tf_op jit(solution)/shard_map/while/body/eval_jaxpr/conv_general_dilated | solution.py:39
  234.2 0.9 dynamic-slice_bitcast_fusion.4
  235.3 21.3 %select_add_fusion.2 = f32[128,128,129]{1,0,2:T(8,128)} fusion(f32[128,128,129]{1,0,2:T(8,128)} %get-tuple-element.216, pred[]{:T(512)S(6)} %compare.6, bf16[128,1,640]{0,1,2:T(2,128)(2,1)S(1)} %copy.17, bf16[128,1,512]{0,1,2:T(2,128)(2,1)S(1)} %copy.18), kind=kOutput, calls=%fused_computation.clone.1 | convolution fusion | flops 2168487936 | bytes 17203200 | tf_op jit(solution)/shard_map/while/body/eval_jaxpr/conv_general_dilated | solution.py:39
  257.7 0.9 dynamic-slice_bitcast_fusion.4
  258.9 21.3 %select_add_fusion.2 = f32[128,128,129]{1,0,2:T(8,128)} fusion(f32[128,128,129]{1,0,2:T(8,128)} %get-tuple-element.216, pred[]{:T(512)S(6)} %compare.6, bf16[128,1,640]{0,1,2:T(2,128)(2,1)S(1)} %copy.17, bf16[128,1,512]{0,1,2:T(2,128)(2,1)S(1)} %copy.18), kind=kOutput, calls=%fused_computation.clone.1 | convolution fusion | flops 2168487936 | bytes 17203200 | tf_op jit(solution)/shard_map/while/body/eval_jaxpr/conv_general_dilated | solution.py:39
  280.2 9.0 %copy.14 = f32[128,128,129]{0,1,2:T(8,128)} copy(f32[128,128,129]{1,0,2:T(8,128)} %get-tuple-element.84) | data formatting | bytes 16908288 | tf_op jit(solution)/shard_map/while | solution.py:50
  289.2 8.5 %multiply_bitcast_fusion = f32[128,129,128]{2,0,1:T(8,128)} fusion(f32[128,128,129]{0,1,2:T(8,128)} %copy.14), kind=kLoop, calls=%fused_computation.3 | loop fusion | flops 2113536 | bytes 16908288 | tf_op jit(solution)/shard_map/mul | solution.py:96
  297.7 99.8 %reduce-scatter.2.cloned.1.call-done = f32[64,129,128]{2,0,1:T(8,128)} async-done(((f32[128,129,128]{2,0,1:T(8,128)}), f32[64,129,128]{2,0,1:T(8,128)}) %reduce-scatter.2.cloned.1.call-update) | async-done | bytes 4227088 | tf_op jit(solution)/shard_map/reduce_scatter | solution.py:95
  (36 shorter events, 12.0 us)
Async XLA Ops:
  6.5 84.7 %all-gather.2.cloned.1.call-start = ((), (), s32[]{:S(2)}) async-start(), calls=%async_computation.1 | async-start | bytes 1179648 | tf_op jit(solution)/shard_map/all_gather | solution.py:87
  7.5 11.6 %collective-permute-start.1 = (f32[128,96]{1,0:T(8,128)S(1)}, f32[128,96]{1,0:T(8,128)S(1)}, u32[]{:S(2)}, u32[]{:S(2)}) collective-permute-start(f32[128,96]{1,0:T(8,128)S(1)} %get-tuple-element.114), channel_id=1, source_target_pairs={{2,0},{3,1},{6,4},{7,5},{10,8},{11,9},{14,12},{15,13},{18,16},{19,... | collective-permute-start | bytes 147464 | tf_op jit(solution)/shard_map/ppermute | solution.py:18
  8.8 10.3 %collective-permute-start = (f32[128,96]{1,0:T(8,128)S(1)}, f32[128,96]{1,0:T(8,128)S(1)}, u32[]{:S(2)}, u32[]{:S(2)}) collective-permute-start(f32[128,96]{1,0:T(8,128)S(1)} %get-tuple-element.115), channel_id=1, source_target_pairs={{0,2},{1,3},{4,6},{5,7},{8,10},{9,11},{12,14},{13,15},{16,18},{17,... | collective-permute-start | bytes 147464 | tf_op jit(solution)/shard_map/ppermute | solution.py:15
  67.4 330.1 %reduce-scatter.2.cloned.1.call-start = ((), (), s32[]{:S(2)}) async-start(), calls=%async_computation.2 | async-start | bytes 12681216 | tf_op jit(solution)/shard_map/reduce_scatter | solution.py:95
Sparse Core Ops, SparseCore 0:
  67.5 23.6 all-gather.1
  297.8 99.6 reduce-scatter.1
where the time goes:
time: 405 us; the launch traced here: 404 us
  matrix products  173 us (43%)
  waiting for transfers between devices  123 us (30%)
  other arithmetic  52.9 us (13%)
  local copies, waits for them, and re-layouts  34.5 us (9%)
  between operations  13.5 us (3%)
  starting transfers between devices  6.39 us (2%)
    conv_general_dilated x8, matrix products, advance(): lax.conv_general_dilated(window[:, None, :], rows_here[:, None, :], (1,),...  168 us
    reduce_scatter x1, waiting for transfers between devices, on_device(): lax.psum_scatter(jnp.transpose(summed[:, :, ::-1], (1, 2, 0)) * norm_scal...  99.8 us
    convert_element_type x1, other arithmetic, on_device(): padded = jnp.where(inside[None, :], whitened_ext, 0.0).astype(jnp.bfloat16)  42.9 us
    all_gather x1, waiting for transfers between devices, on_device(): segment = lax.all_gather(slot_rows, ('chan', 'sub'), axis=0, tiled=True)  23.6 us
    broadcast_in_dim x16, local copies, waits for them, and re-layouts, advance(): window[:, None, :]  9.16 us
    while x1, local copies, waits for them, and re-layouts, correlate(): return lax.fori_loop(0, block_count, advance, start_sum)  9 us
    broadcast_in_dim x16, local copies, waits for them, and re-layouts, advance(): rows_here[:, None, :]  8.59 us
    mul x1, other arithmetic, on_device(): jnp.transpose(summed[:, :, ::-1], (1, 2, 0)) * norm_scale  8.51 us
  transfers between devices with their start and end apart: 4, of which 2 were waited for; matrix products, arithmetic and copies ran while one was open for 1% of the time, Pallas kernels for 0%

commit v1 on v0

--- a/solution.py
+++ b/solution.py
@@ -3,8 +3,26 @@
 import jax.numpy as jnp
 from jax import lax
 from jax.sharding import PartitionSpec as P
+from jax.lax import axis_index, axis_size, ppermute
 
 LAGS = 129
+
+
+def _play_scenes(view, in_dim):
+    view = jnp.moveaxis(view, 0, in_dim)
+    e_now = view.shape
+    return view.reshape(*e_now[:in_dim], e_now[in_dim] * e_now[in_dim + 1], *e_now[in_dim + 2 :])
+
+
+def advance_the_face(work_x, device_axis):
+    then, part_next = (axis_size(device_axis), axis_index(device_axis))
+    h_now, tall = (work_x[None], 1)
+    while tall < then:
+        spare = ppermute(h_now, device_axis, list(map(lambda p: (p, p ^ tall), range(then))))
+        y2 = part_next & tall == 0
+        h_now = jnp.concatenate([jnp.where(y2, h_now, spare), jnp.where(y2, spare, h_now)])
+        tall *= 2
+    return h_now
 
 
 def padded_2(block, sides, width):
@@ -84,7 +102,7 @@
     picker = jnp.dot(choose, onehot, preferred_element_type=jnp.float32).astype(jnp.bfloat16)
     slot_rows = jnp.dot(picker, whitened, preferred_element_type=jnp.float32).astype(jnp.bfloat16)
     slot_id = owners * slot_most + rank_in
-    segment = lax.all_gather(slot_rows, ("chan", "sub"), axis=0, tiled=True)
+    segment = _play_scenes(advance_the_face(slot_rows, ("chan", "sub")), 0)
     row_count = segment.shape[0]
     select = (slot_id[:, None] == jnp.arange(row_count, dtype=jnp.int32)[None, :]).astype(
         jnp.bfloat16

time: 405 us -> 417 us (1.030)
  waiting for transfers between devices: 123 us -> 131 us
  starting transfers between devices: 6.39 us -> 11.8 us
    ppermute x0 -> x3, waiting for transfers between devices: none -> 30.7 us  [advance_the_face(): ppermute(h_now, device_axis, list(map(lambda p: (p, p ^ tall), range(then...]
    all_gather x1 -> x0, waiting for transfers between devices: 23.6 us -> none  [on_device(): segment = lax.all_gather(slot_rows, ('chan', 'sub'), axis=0, tiled=True)]
    ppermute x0 -> x3, starting transfers between devices: none -> 5.65 us  [advance_the_face(): ppermute(h_now, device_axis, list(map(lambda p: (p, p ^ tall), range(then...]
  transfers between devices with their start and end apart: 4 -> 6, of which waited for: 2 -> 4; matrix products, arithmetic and copies ran while one was open for 1% -> 1% of each run, Pallas kernels for 0% -> 0%
where the time goes in v1:
time: 417 us; the launch traced here: 416 us
  matrix products  172 us (41%)
  waiting for transfers between devices  131 us (31%)
  other arithmetic  53.2 us (13%)
  local copies, waits for them, and re-layouts  34.5 us (8%)
  between operations  13.5 us (3%)
  starting transfers between devices  11.8 us (3%)
    conv_general_dilated x8, matrix products, advance(): lax.conv_general_dilated(window[:, None, :], rows_here[:, None, :], (1,),...  168 us
    reduce_scatter x1, waiting for transfers between devices, on_device(): lax.psum_scatter(jnp.transpose(summed[:, :, ::-1], (1, 2, 0)) * norm_scal...  100 us
    convert_element_type x1, other arithmetic, on_device(): padded = jnp.where(inside[None, :], whitened_ext, 0.0).astype(jnp.bfloat16)  42.9 us
    ppermute x3, waiting for transfers between devices, advance_the_face(): ppermute(h_now, device_axis, list(map(lambda p: (p, p ^ tall), range(then...  30.7 us
    broadcast_in_dim x16, local copies, waits for them, and re-layouts, advance(): window[:, None, :]  9.16 us
    while x1, local copies, waits for them, and re-layouts, correlate(): return lax.fori_loop(0, block_count, advance, start_sum)  8.99 us
    broadcast_in_dim x16, local copies, waits for them, and re-layouts, advance(): rows_here[:, None, :]  8.59 us
    mul x1, other arithmetic, on_device(): jnp.transpose(summed[:, :, ::-1], (1, 2, 0)) * norm_scale  8.52 us
  transfers between devices with their start and end apart: 6, of which 4 were waited for; matrix products, arithmetic and copies ran while one was open for 1% of the time, Pallas kernels for 0%

profile of v1, /device:TPU:0, one launch (start us, length us, event | category | flops | bytes accessed | tf_op | source)
XLA Modules:
  0.0 415.8 jit_solution(26174954267684269)
XLA Ops:
  6.5 1.0 fusion.82
  7.5 1.3 collective-permute-start.1
  8.8 4.9 %collective-permute-start = (f32[128,96]{1,0:T(8,128)S(1)}, f32[128,96]{1,0:T(8,128)S(1)}, u32[]{:S(2)}, u32[]{:S(2)}) collective-permute-start(f32[128,96]{1,0:T(8,128)S(1)} %get-tuple-element.115), channel_id=1, source_target_pairs={{0,2},{1,3},{4,6},{5,7},{8,10},{9,11},{12,14},{13,15},{16,18},{17,... | collective-permute-start | bytes 147464 | tf_op jit(solution)/shard_map/ppermute | solution.py:33
  14.6 1.0 slice_bitcast_fusion.63
  15.6 1.0 slice_bitcast_fusion.64
  16.6 1.0 slice_bitcast_fusion.62
  19.1 2.9 concatenate.12
  22.1 42.9 %fusion.3 = bf16[128,4224]{1,0:T(8,128)(2,1)} fusion(f32[128,4288]{1,0:T(8,128)S(1)} %concatenate.12, f32[128]{0:T(128)S(1)} %get-tuple-element.185, f32[128]{0:T(128)S(1)} %get-tuple-element.186, f32[128]{0:T(128)S(1)} %get-tuple-element.123, f32[128]{0:T(128)S(1)} %get-tuple-element.124, f32[128]{0:T(128)S(1)} %get-tuple-element.125, ...), kind=kLoop, calls=%fused_computation.10 | loop fusion | flops 70828032 | bytes 141693568 | tf_op jit(solution)/shard_map/convert_element_type | solution.py:86
  65.0 1.7 fusion
  66.8 1.3 collective-permute-done.2
  68.2 2.8 collective-permute-start.3
  70.9 6.6 %collective-permute-done.3 = bf16[2,16,4096]{2,1,0:T(8,128)(2,1)S(1)} collective-permute-done((bf16[2,16,4096]{2,1,0:T(8,128)(2,1)S(1)}, bf16[2,16,4096]{2,1,0:T(8,128)(2,1)S(1)}, u32[]{:S(2)}, u32[]{:S(2)}) %collective-permute-start.3) | collective-permute-done | bytes 262176 | tf_op jit(solution)/shard_map/ppermute | solution.py:21
  77.7 2.8 collective-permute-start.4
  80.5 22.8 %collective-permute-done.4 = bf16[4,16,4096]{2,1,0:T(8,128)(2,1)S(1)} collective-permute-done((bf16[4,16,4096]{2,1,0:T(8,128)(2,1)S(1)}, bf16[4,16,4096]{2,1,0:T(8,128)(2,1)S(1)}, u32[]{:S(2)}, u32[]{:S(2)}) %collective-permute-start.4) | collective-permute-done | bytes 524320 | tf_op jit(solution)/shard_map/ppermute | solution.py:21
  103.4 1.5 convolution_convert_fusion
  105.0 186.2 %while.14 = (s32[]{:T(128)}, f32[128,128,129]{1,0,2:T(8,128)}, bf16[128,4224]{1,0:T(8,128)(2,1)}, bf16[128,4096]{1,0:T(8,128)(2,1)}, s32[]{:T(128)}, /*index=5*/s32[]{:T(128)}, s32[]{:T(128)}, s32[]{:T(128)}, s32[]{:T(128)}) while((s32[]{:T(128)}, f32[128,128,129]{1,0,2:T(8,128)}, bf16[128,4224]{1,0:T(8,128)(2,1)}, ...), condition=%wide.region_2.3_spmd.clone, body=%wide.region_1.2_spmd.clone.sunk | while | flops 2168487936 | bytes 18383036 | solution.py:68
  106.1 0.9 dynamic-slice_bitcast_fusion.4
  107.2 19.1 %select_add_fusion.2 = f32[128,128,129]{1,0,2:T(8,128)} fusion(f32[128,128,129]{1,0,2:T(8,128)} %get-tuple-element.222, pred[]{:T(512)S(6)} %compare.6, bf16[128,1,640]{0,1,2:T(2,128)(2,1)S(1)} %copy.17, bf16[128,1,512]{0,1,2:T(2,128)(2,1)S(1)} %copy.18), kind=kOutput, calls=%fused_computation.clone.1 | convolution fusion | flops 2168487936 | bytes 17203200 | tf_op jit(solution)/shard_map/while/body/eval_jaxpr/conv_general_dilated | solution.py:57
  127.4 0.9 dynamic-slice_bitcast_fusion.4
  128.6 21.3 %select_add_fusion.2 = f32[128,128,129]{1,0,2:T(8,128)} fusion(f32[128,128,129]{1,0,2:T(8,128)} %get-tuple-element.222, pred[]{:T(512)S(6)} %compare.6, bf16[128,1,640]{0,1,2:T(2,128)(2,1)S(1)} %copy.17, bf16[128,1,512]{0,1,2:T(2,128)(2,1)S(1)} %copy.18), kind=kOutput, calls=%fused_computation.clone.1 | convolution fusion | flops 2168487936 | bytes 17203200 | tf_op jit(solution)/shard_map/while/body/eval_jaxpr/conv_general_dilated | solution.py:57
  151.0 0.9 dynamic-slice_bitcast_fusion.4
  152.1 21.3 %select_add_fusion.2 = f32[128,128,129]{1,0,2:T(8,128)} fusion(f32[128,128,129]{1,0,2:T(8,128)} %get-tuple-element.222, pred[]{:T(512)S(6)} %compare.6, bf16[128,1,640]{0,1,2:T(2,128)(2,1)S(1)} %copy.17, bf16[128,1,512]{0,1,2:T(2,128)(2,1)S(1)} %copy.18), kind=kOutput, calls=%fused_computation.clone.1 | convolution fusion | flops 2168487936 | bytes 17203200 | tf_op jit(solution)/shard_map/while/body/eval_jaxpr/conv_general_dilated | solution.py:57
  174.5 0.9 dynamic-slice_bitcast_fusion.4
  175.7 21.3 %select_add_fusion.2 = f32[128,128,129]{1,0,2:T(8,128)} fusion(f32[128,128,129]{1,0,2:T(8,128)} %get-tuple-element.222, pred[]{:T(512)S(6)} %compare.6, bf16[128,1,640]{0,1,2:T(2,128)(2,1)S(1)} %copy.17, bf16[128,1,512]{0,1,2:T(2,128)(2,1)S(1)} %copy.18), kind=kOutput, calls=%fused_computation.clone.1 | convolution fusion | flops 2168487936 | bytes 17203200 | tf_op jit(solution)/shard_map/while/body/eval_jaxpr/conv_general_dilated | solution.py:57
  198.1 0.9 dynamic-slice_bitcast_fusion.4
  199.2 21.3 %select_add_fusion.2 = f32[128,128,129]{1,0,2:T(8,128)} fusion(f32[128,128,129]{1,0,2:T(8,128)} %get-tuple-element.222, pred[]{:T(512)S(6)} %compare.6, bf16[128,1,640]{0,1,2:T(2,128)(2,1)S(1)} %copy.17, bf16[128,1,512]{0,1,2:T(2,128)(2,1)S(1)} %copy.18), kind=kOutput, calls=%fused_computation.clone.1 | convolution fusion | flops 2168487936 | bytes 17203200 | tf_op jit(solution)/shard_map/while/body/eval_jaxpr/conv_general_dilated | solution.py:57
  222.8 21.3 %select_add_fusion.2 = f32[128,128,129]{1,0,2:T(8,128)} fusion(f32[128,128,129]{1,0,2:T(8,128)} %get-tuple-element.222, pred[]{:T(512)S(6)} %compare.6, bf16[128,1,640]{0,1,2:T(2,128)(2,1)S(1)} %copy.17, bf16[128,1,512]{0,1,2:T(2,128)(2,1)S(1)} %copy.18), kind=kOutput, calls=%fused_computation.clone.1 | convolution fusion | flops 2168487936 | bytes 17203200 | tf_op jit(solution)/shard_map/while/body/eval_jaxpr/conv_general_dilated | solution.py:57
  246.3 21.3 %select_add_fusion.2 = f32[128,128,129]{1,0,2:T(8,128)} fusion(f32[128,128,129]{1,0,2:T(8,128)} %get-tuple-element.222, pred[]{:T(512)S(6)} %compare.6, bf16[128,1,640]{0,1,2:T(2,128)(2,1)S(1)} %copy.17, bf16[128,1,512]{0,1,2:T(2,128)(2,1)S(1)} %copy.18), kind=kOutput, calls=%fused_computation.clone.1 | convolution fusion | flops 2168487936 | bytes 17203200 | tf_op jit(solution)/shard_map/while/body/eval_jaxpr/conv_general_dilated | solution.py:57
  269.9 21.3 %select_add_fusion.2 = f32[128,128,129]{1,0,2:T(8,128)} fusion(f32[128,128,129]{1,0,2:T(8,128)} %get-tuple-element.222, pred[]{:T(512)S(6)} %compare.6, bf16[128,1,640]{0,1,2:T(2,128)(2,1)S(1)} %copy.17, bf16[128,1,512]{0,1,2:T(2,128)(2,1)S(1)} %copy.18), kind=kOutput, calls=%fused_computation.clone.1 | convolution fusion | flops 2168487936 | bytes 17203200 | tf_op jit(solution)/shard_map/while/body/eval_jaxpr/conv_general_dilated | solution.py:57
  291.2 9.0 %copy.14 = f32[128,128,129]{0,1,2:T(8,128)} copy(f32[128,128,129]{1,0,2:T(8,128)} %get-tuple-element.84) | data formatting | bytes 16908288 | tf_op jit(solution)/shard_map/while | solution.py:68
  300.1 8.5 %multiply_bitcast_fusion = f32[128,129,128]{2,0,1:T(8,128)} fusion(f32[128,128,129]{0,1,2:T(8,128)} %copy.14), kind=kLoop, calls=%fused_computation.3 | loop fusion | flops 2113536 | bytes 16908288 | tf_op jit(solution)/shard_map/mul | solution.py:114
  308.7 100.3 %reduce-scatter.2.cloned.1.call-done = f32[64,129,128]{2,0,1:T(8,128)} async-done(((f32[128,129,128]{2,0,1:T(8,128)}), f32[64,129,128]{2,0,1:T(8,128)}) %reduce-scatter.2.cloned.1.call-update) | async-done | bytes 4227088 | tf_op jit(solution)/shard_map/reduce_scatter | solution.py:113
  (45 shorter events, 15.8 us)
Async XLA Ops:
  6.5 402.4 %reduce-scatter.2.cloned.1.call-start = ((), (), s32[]{:S(2)}) async-start(), calls=%async_computation.1 | async-start | bytes 12681216 | tf_op jit(solution)/shard_map/reduce_scatter | solution.py:113
  7.5 11.6 %collective-permute-start.1 = (f32[128,96]{1,0:T(8,128)S(1)}, f32[128,96]{1,0:T(8,128)S(1)}, u32[]{:S(2)}, u32[]{:S(2)}) collective-permute-start(f32[128,96]{1,0:T(8,128)S(1)} %get-tuple-element.114), channel_id=1, source_target_pairs={{2,0},{3,1},{6,4},{7,5},{10,8},{11,9},{14,12},{15,13},{18,16},{19,... | collective-permute-start | bytes 147464 | tf_op jit(solution)/shard_map/ppermute | solution.py:36
  8.8 10.3 %collective-permute-start = (f32[128,96]{1,0:T(8,128)S(1)}, f32[128,96]{1,0:T(8,128)S(1)}, u32[]{:S(2)}, u32[]{:S(2)}) collective-permute-start(f32[128,96]{1,0:T(8,128)S(1)} %get-tuple-element.115), channel_id=1, source_target_pairs={{0,2},{1,3},{4,6},{5,7},{8,10},{9,11},{12,14},{13,15},{16,18},{17,... | collective-permute-start | bytes 147464 | tf_op jit(solution)/shard_map/ppermute | solution.py:33
  66.7 1.4 collective-permute-start.2
  68.2 9.4 %collective-permute-start.3 = (bf16[2,16,4096]{2,1,0:T(8,128)(2,1)S(1)}, bf16[2,16,4096]{2,1,0:T(8,128)(2,1)S(1)}, u32[]{:S(2)}, u32[]{:S(2)}) collective-permute-start(bf16[2,16,4096]{2,1,0:T(8,128)(2,1)S(1)} %pad_maximum_fusion.2), channel_id=1, source_target_pairs={{0,4},{1,5},{4,0},{5,1},{8,12},{9,13},{12,8},{13,9},{2,6},{3,7},{6... | collective-permute-start | bytes 786440 | tf_op jit(solution)/shard_map/ppermute | solution.py:21
  77.7 25.6 %collective-permute-start.4 = (bf16[4,16,4096]{2,1,0:T(8,128)(2,1)S(1)}, bf16[4,16,4096]{2,1,0:T(8,128)(2,1)S(1)}, u32[]{:S(2)}, u32[]{:S(2)}) collective-permute-start(bf16[4,16,4096]{2,1,0:T(8,128)(2,1)S(1)} %pad_maximum_fusion.1), channel_id=1, source_target_pairs={{0,8},{1,9},{4,12},{5,13},{8,0},{9,1},{12,4},{13,5},{2,10},{3,11},... | collective-permute-start | bytes 1572872 | tf_op jit(solution)/shard_map/ppermute | solution.py:21
Sparse Core Ops, SparseCore 0:
  308.8 100.1 reduce-scatter.1
